TPU v7x, 256 devices: a whole 4x4x8 slice. The times are simulated.
256 devices in a mesh: seq: 32 (over z, y), mp: 4 (over x), req: 2 (over core).
Axes of the slice: x: 4, y: 4, z: 8, core: 2. Of those that a mesh axis runs over, the one named last changes fastest.
Arguments:
- hidden: bfloat16 [2, 8192, 3072], P('req', 'seq', 'mp'), may hold values from -6 to 6
- norm_gain: bfloat16 [3072], replicated, may hold values from 0.5 to 1.5
- w_query: bfloat16 [3072, 1024], P(None, 'mp'), may hold values from -0.109375 to 0.109375
- w_keyval: bfloat16 [3072, 512], P(None, 'mp'), may hold values from -0.109375 to 0.109375
- w_attn_out: bfloat16 [1024, 3072], P('mp'), may hold values from -1.5 to 1.5
- w_inner: bfloat16 [3072, 2, 1536], P(None, None, 'mp'), may hold values from -0.109375 to 0.109375
- w_bc: bfloat16 [3072, 512], P(None, 'mp'), may hold values from -0.109375 to 0.109375
- w_dt: bfloat16 [3072, 12], P(None, 'mp'), may hold values from -0.109375 to 0.109375
- dt_bias: float32 [12], P('mp'), may hold values from -4 to 0
- a_log: float32 [12], P('mp'), may hold values from -12 to 0
- d_skip: float32 [12], P('mp'), may hold values from 0.1 to 10
- conv_x: bfloat16 [4, 1536], P(None, 'mp'), may hold values from -3 to 3
- conv_bc: bfloat16 [4, 512], replicated, may hold values from -3 to 3
- mamba_gain: bfloat16 [1536], P('mp'), may hold values from 0.5 to 1.5
- w_mamba_out: bfloat16 [1536, 3072], P('mp'), may hold values from -0.15625 to 0.15625
- cache: bfloat16 [2, 8192, 512], P('req', 'seq', 'mp'), may hold values from -70 to 70, as said below
- cache_len: int32 [2], P('req'), may hold values from 256 to 8192
- tail_x: bfloat16 [2, 3, 1536], P('req', None, 'mp'), may hold values from -6 to 6
- tail_bc: bfloat16 [2, 3, 512], P('req'), may hold values from -6 to 6
- ssm_init: float32 [2, 12, 128, 256], P('req', 'mp'), may hold values from -6 to 6
Outputs:
- layer_out: bfloat16 [2, 8192, 3072], P('req', 'seq', 'mp')
- new_keyval: bfloat16 [2, 8192, 512], P('req', 'seq', 'mp')
- block_states: float32 [2, 32, 12, 128, 256], P('req', 'seq', 'mp')
Inputs may be any that keep to these rules, and one draw needn't show every extreme that they name: Rows of the cache at or past cache_len are unused.
All inputs are finite; a program needn't handle non-finite values.
Results may differ from a plain program's by a relative error of at most 0.0097.
Values may be sent and summed in bfloat16 or wider, within the bound.
A program may use at most 192 MiB of HBM per device.

v0:
```python
import jax
import jax.numpy as jnp
from jax import lax
from jax.sharding import PartitionSpec as P

HD = 128
QH = 8
KVH = 2
NS = 256
CONV = 4
epsilon = 1e-05
rope_base = 100000000000.0
negative = -1e30


def shifted(block, axis, distance):
    devices = range(lax.axis_size(axis))
    route = [(i - distance, i) for i in devices if i - distance in devices]
    return lax.ppermute(block, axis, route)


def prefix(part, axis, combine, identity):
    place = lax.axis_index(axis)
    gathered = jax.tree.map(lambda a: lax.all_gather(a, axis), part)
    state = jax.tree.map(lambda a, e: jnp.zeros_like(a) + jnp.asarray(e, a.dtype), part, identity)

    def one(turn, state):
        return combine(
            state, jax.tree.map(lambda a: lax.dynamic_index_in_dim(a, turn, 0, False), gathered)
        )

    return lax.fori_loop(0, place, one, state)


def rotate(values, positions):
    half = HD // 2
    freqs = rope_base ** (-jnp.arange(half, dtype=jnp.float32) * 2.0 / HD)
    angles = positions.astype(jnp.float32)[:, None] * freqs[None, :]
    cosine = jnp.cos(angles)[:, None, :]
    sine = jnp.sin(angles)[:, None, :]
    first = values[..., :half]
    second = values[..., half:]
    return jnp.concatenate(
        [first * cosine - second * sine, second * cosine + first * sine], axis=-1
    )


def rms_scale(values):
    mean_sq = jnp.mean(values * values, axis=-1, keepdims=True)
    return values * lax.rsqrt(mean_sq + epsilon)


def causal_conv(tail, inputs, taps):
    padded = jnp.concatenate([tail, inputs], axis=0).astype(jnp.float32)
    count = inputs.shape[0]
    total = jnp.zeros(inputs.shape, jnp.float32)
    for offset in range(CONV):
        total = total + taps[offset].astype(jnp.float32)[None, :] * padded[offset : offset + count]
    return jax.nn.silu(total)


def join_states(earlier, later):
    return (earlier[0] * later[0], later[0][:, None, None] * earlier[1] + later[1])


def shards(
    hidden,
    norm_gain,
    w_query,
    w_keyval,
    w_attn_out,
    w_inner,
    w_bc,
    w_dt,
    dt_bias,
    a_log,
    d_skip,
    conv_x,
    conv_bc,
    mamba_gain,
    w_mamba_out,
    cache,
    cache_len,
    tail_x,
    tail_bc,
    ssm_init,
):
    high = lax.Precision.HIGHEST
    own_rows = hidden[0]
    tokens = own_rows.shape[0]
    seq_pos = lax.axis_index("seq")
    mp_pos = lax.axis_index("mp")
    length = cache_len[0]
    whole = lax.all_gather(own_rows, "mp", axis=1, tiled=True)
    normed = (rms_scale(whole.astype(jnp.float32)) * norm_gain.astype(jnp.float32)).astype(
        jnp.bfloat16
    )
    positions = length + seq_pos * tokens + jnp.arange(tokens, dtype=jnp.int32)
    local_heads = w_query.shape[1] // HD
    query = rotate(
        jnp.dot(normed, w_query, preferred_element_type=jnp.float32).reshape(
            tokens, local_heads, HD
        ),
        positions,
    ).astype(jnp.bfloat16)
    projected = jnp.dot(normed, w_keyval, preferred_element_type=jnp.float32)
    roped = rotate(projected[:, None, :], positions)[:, 0, :]
    kv_block = jnp.where(mp_pos % 2 == 0, roped, projected).astype(jnp.bfloat16)
    bc_block = jnp.dot(normed, w_bc, preferred_element_type=jnp.float32).astype(jnp.bfloat16)
    kv_all, bc_all, cache_all = (
        lax.all_gather(kv_block, "mp", axis=1, tiled=True),
        lax.all_gather(bc_block, "mp", axis=1, tiled=True),
        lax.all_gather(cache[0], "mp", axis=1, tiled=True),
    )
    inner = jnp.einsum("td,dkc->tkc", normed, w_inner, preferred_element_type=jnp.float32).astype(
        jnp.bfloat16
    )
    rim = CONV - 1
    prev_x, prev_bc = shifted((inner[tokens - rim :, 1], bc_all[tokens - rim :]), "seq", 1)
    first_block = seq_pos == 0
    prev_x = jnp.where(first_block, tail_x[0], prev_x)
    prev_bc = jnp.where(first_block, tail_bc[0], prev_bc)
    mamba_heads = dt_bias.shape[0]
    x_conv = causal_conv(prev_x, inner[:, 1], conv_x).reshape(tokens, mamba_heads, HD)
    bc_conv = causal_conv(prev_bc, bc_all, conv_bc)
    b_mat = bc_conv[:, :NS]
    c_mat = bc_conv[:, NS:]
    step_size = jax.nn.softplus(jnp.dot(normed, w_dt, preferred_element_type=jnp.float32) + dt_bias)
    log_decay = -step_size * jnp.exp(a_log)[None, :]
    cumulative = jnp.cumsum(log_decay, axis=0)
    pairs = jnp.dot(c_mat, b_mat.T, precision=high)
    gap = cumulative[:, None, :] - cumulative[None, :, :]
    token_ids = jnp.arange(tokens)
    lower = (token_ids[:, None] >= token_ids[None, :])[:, :, None]
    decay = jnp.where(lower, jnp.exp(jnp.where(lower, gap, 0.0)), 0.0)
    mixing = decay * pairs[:, :, None] * step_size[None, :, :]
    inner_out = jnp.einsum("tsh,shp->thp", mixing, x_conv, precision=high)
    to_end = jnp.exp(cumulative[-1][None, :] - cumulative) * step_size
    own_state = jnp.einsum("sh,shp,sn->hpn", to_end, x_conv, b_mat, precision=high)
    block_decay = jnp.exp(cumulative[-1])
    prior_decay, prior_state = prefix(
        (block_decay, own_state),
        "seq",
        join_states,
        (jnp.ones_like(block_decay), jnp.zeros_like(own_state)),
    )
    incoming = prior_state + prior_decay[:, None, None] * ssm_init[0]
    carried = jnp.exp(cumulative)[:, :, None] * jnp.einsum(
        "tn,hpn->thp", c_mat, incoming, precision=high
    )
    mamba_y = inner_out + carried + d_skip[None, :, None] * x_conv
    state_after = block_decay[:, None, None] * incoming + own_state
    gated = mamba_y * jax.nn.silu(inner[:, 0].astype(jnp.float32).reshape(tokens, mamba_heads, HD))
    mixed = (
        rms_scale(gated).reshape(tokens, mamba_heads * HD) * mamba_gain.astype(jnp.float32)
    ).astype(jnp.bfloat16)
    cache_rows = cache_all.shape[0]
    shard_rows = cache_rows + tokens
    local_rows = jnp.concatenate([cache_all, kv_all], axis=0)
    group = mp_pos * local_heads // (QH // KVH)
    query_index = seq_pos * tokens + jnp.arange(tokens, dtype=jnp.int32)
    scale = 1.0 / float(HD) ** 0.5
    piece = lax.all_gather(local_rows, "seq", axis=0, tiled=True)
    top = jnp.full((local_heads, tokens), negative, jnp.float32)
    piece = lax.dynamic_slice_in_dim(piece, group * 2 * HD, 2 * HD, 1)
    count = piece.shape[0]
    index = jnp.arange(count, dtype=jnp.int32)
    owner = index // shard_rows
    offset = index % shard_rows
    in_cache = offset < cache_rows
    slot_ok = in_cache & (owner * cache_rows + offset < length)
    new_index = owner * tokens + offset - cache_rows
    valid = slot_ok[None, :] | (~in_cache)[None, :] & (new_index[None, :] <= query_index[:, None])
    scores = (
        jnp.einsum("qhd,kd->hqk", query, piece[:, :HD], preferred_element_type=jnp.float32) * scale
    )
    masked = jnp.where(valid[None], scores, negative)
    new_top = jnp.maximum(top, jnp.max(masked, axis=-1))
    weights = jnp.where(valid[None], jnp.exp(masked - new_top[:, :, None]), 0.0)
    total = jnp.sum(weights, axis=-1)
    accum = jnp.einsum(
        "hqk,kd->hqd",
        weights.astype(jnp.bfloat16),
        piece[:, HD : 2 * HD],
        preferred_element_type=jnp.float32,
    )
    top, total, accum = (new_top, total, accum)
    attended = jnp.transpose(accum / total[:, :, None], (1, 0, 2)).reshape(tokens, local_heads * HD)
    attended = attended.astype(jnp.bfloat16)
    term = jnp.dot(attended, w_attn_out, preferred_element_type=jnp.float32)
    term = term + jnp.dot(mixed, w_mamba_out, preferred_element_type=jnp.float32)
    summed = lax.psum_scatter(term, "mp", scatter_dimension=1, tiled=True)
    layer = (summed + own_rows.astype(jnp.float32)).astype(jnp.bfloat16)
    return (layer[None], kv_block[None], state_after[None, None])


def solution(mesh):
    placed = (
        P("req", "seq", "mp"),
        P(),
        P(None, "mp"),
        P(None, "mp"),
        P("mp", None),
        P(None, None, "mp"),
        P(None, "mp"),
        P(None, "mp"),
        P("mp"),
        P("mp"),
        P("mp"),
        P(None, "mp"),
        P(),
        P("mp"),
        P("mp", None),
        P("req", "seq", "mp"),
        P("req"),
        P("req", None, "mp"),
        P("req", None, None),
        P("req", "mp", None, None),
    )
    return jax.shard_map(
        shards,
        mesh=mesh,
        in_specs=placed,
        out_specs=(P("req", "seq", "mp"), P("req", "seq", "mp"), P("req", "seq", "mp", None, None)),
        check_vma=False,
    )
```

profile of v0, /device:TPU:1, one launch (start us, length us, event | category | flops | bytes accessed | tf_op | source)
XLA Modules:
  0.0 449.3 jit_solution(8750988892536039679)
XLA Ops:
  11.0 31.7 %all-gather.10.cloned.1.call-done = bf16[1,256,3072]{2,1,0:T(8,128)(2,1)} async-done(((bf16[1,256,768]{2,1,0:T(8,128)(2,1)}), bf16[1,256,3072]{2,1,0:T(8,128)(2,1)}) %all-gather.10.cloned.1.call-update) | async-done | bytes 1572880 | tf_op jit(solution)/shard_map/all_gather | solution.py:94
  42.7 1.9 fusion.9
  44.7 1.9 fusion.11
  46.6 1.4 fusion.13
  51.6 3.1 collective-permute-start
  54.7 2.0 convolution_convert_fusion
  56.7 9.4 %all_gather.29 = bf16[256,512]{1,0:T(8,128)(2,1)S(1)} all-gather(bf16[256,128]{1,0:T(8,128)(2,1)S(1)} %convolution_convert_fusion), channel_id=1, replica_groups=mesh['seq'=32,'mp'=4,'req'=2] {'mp'}, dimensions={1}, use_global_device_ids=true | all-gather | bytes 327680 | tf_op jit(solution)/shard_map/all_gather | solution.py:112
  66.1 3.2 collective-permute-start.1
  69.9 1.0 maximum_convert_fusion.1
  71.8 1.3 fusion.46
  73.9 9.4 %all-gather = bf16[1,256,512]{1,2,0:T(8,128)(2,1)S(1)} all-gather(bf16[1,256,128]{1,2,0:T(8,128)(2,1)S(1)} %copy.52), channel_id=2, replica_groups=mesh['seq'=32,'mp'=4,'req'=2] {'mp'}, dimensions={2}, use_global_device_ids=true | all-gather | bytes 327680 | tf_op jit(solution)/shard_map/all_gather | solution.py:113
  83.3 2.3 fusion.100
  85.9 9.8 %all_gather.27 = bf16[256,512]{0,1:T(8,128)(2,1)S(1)} all-gather(bf16[256,128]{0,1:T(8,128)(2,1)S(1)} %fusion.63), channel_id=1, replica_groups=mesh['seq'=32,'mp'=4,'req'=2] {'mp'}, dimensions={1}, use_global_device_ids=true | all-gather | bytes 327680 | tf_op jit(solution)/shard_map/all_gather | solution.py:111
  97.4 1.3 multiply_cosine_fusion
  98.6 15.5 %and_or_fusion = pred[256,16384]{0,1:T(8,128)(4,1)} fusion(s32[256]{0:T(256)S(1)} %iota_add_fusion, s32[16384]{0:T(1024)S(1)} %fusion.82, pred[16384]{0:T(1024)(128)(4,1)S(1)} %get-tuple-element.110, pred[16384]{0:T(1024)(128)(4,1)S(1)} %get-tuple-element.109), kind=kLoop, calls=%fused_computation.9 | loop fusion | flops 12582912 | bytes 4293632 | tf_op jit(solution)/shard_map/or | solution.py:173
  114.1 1.9 copy.63
  116.0 2.6 fusion.101
  119.0 37.4 %all-gather.3 = f32[32,1,3]{2,1,0:T(1,128)} all-gather(f32[1,1,3]{2,1,0:T(1,128)S(1)} %bitcast.181), channel_id=1, replica_groups=mesh['seq'=32,'mp'=4,'req'=2] {'seq'}, dimensions={0}, use_global_device_ids=true | all-gather | bytes 396 | tf_op jit(solution)/shard_map/all_gather | solution.py:24
  156.4 1.7 subtract_convert_fusion
  158.5 39.1 %all-gather.12.cloned.1.call-done = f32[96,128,256]{2,1,0:T(8,128)} async-done(((f32[3,128,256]{2,1,0:T(8,128)}), f32[96,128,256]{2,1,0:T(8,128)}) %all-gather.12.cloned.1.call-update) | async-done | bytes 12582928 | tf_op jit(solution)/shard_map/all_gather | solution.py:24
  197.7 1.5 convolution_multiply_fusion
  199.2 2.5 multiply_reduce_fusion
  201.9 143.7 %all-gather.8.cloned.1.call-done = bf16[16384,512]{0,1:T(8,128)(2,1)} async-done(((bf16[512,512]{0,1:T(8,128)(2,1)}), bf16[16384,512]{0,1:T(8,128)(2,1)}) %all-gather.8.cloned.1.call-update) | async-done | bytes 16777232 | tf_op jit(solution)/shard_map/all_gather | solution.py:163
  345.7 17.5 %fusion = (f32[2,256]{1,0:T(2,128)S(1)}, f32[16384,256,2]{1,0,2:T(8,128)}) fusion(pred[256,16384]{0,1:T(8,128)(4,1)} %and_or_fusion, bf16[256,2,64]{2,0,1:T(8,128)(2,1)S(1)} %copy-done.8, bf16[256,2,64]{2,0,1:T(8,128)(2,1)S(1)} %copy-done.7, bf16[16384,512]{0,1:T(8,128)(2,1)} %all-gather.8.cloned.1.call-done, s32[]{:T(128)S(6)} %select_n.107), kind=kOutput, calls=%fused_computation.4 | convolution fusion | flops 2172911104 | bytes 42076164 | tf_op jit(solution)/shard_map/qhd,kd->hqk/dot_general | solution.py:175
  363.2 15.6 %fusion.1 = f32[2,256]{1,0:T(2,128)S(1)} fusion(f32[16384,256,2]{1,0,2:T(8,128)} %get-tuple-element.104, f32[2,256]{1,0:T(2,128)S(1)} %broadcast_maximum_fusion, pred[256,16384]{0,1:T(8,128)(4,1)} %and_or_fusion), kind=kLoop, calls=%fused_computation.5 | loop fusion | flops 41942528 | bytes 37752832 | tf_op jit(solution)/shard_map/reduce_sum | solution.py:180
  378.8 17.1 %fusion.27 = bf16[256,2,128]{0,2,1:T(8,128)(2,1)S(1)} fusion(f32[16384,256,2]{1,0,2:T(8,128)} %get-tuple-element.104, f32[2,256]{1,0:T(2,128)S(1)} %broadcast_maximum_fusion, pred[256,16384]{0,1:T(8,128)(4,1)} %and_or_fusion, bf16[16384,512]{0,1:T(8,128)(2,1)} %all-gather.8.cloned.1.call-done, s32[]{:T(128)S(6)} %add.229, f32[256,2]{0,1:T(2,128)S(1)} %bitcast.180), kind=kOutput, calls=%fused_computation.32 | convolution fusion | flops 2189557760 | bytes 42078212 | tf_op jit(solution)/shard_map/hqk,kd->hqd/dot_general | solution.py:181
  395.9 2.0 fusion.102
  397.9 2.7 convolution_add_fusion
  400.7 1.6 copy.64
  402.3 1.9 add_bitcast_fusion
  404.2 36.7 %reduce-scatter.2.cloned.1.call-done = f32[256,768]{1,0:T(8,128)} async-done(((f32[256,3072]{1,0:T(8,128)}), f32[256,768]{1,0:T(8,128)}) %reduce-scatter.2.cloned.1.call-update) | async-done | bytes 786448 | tf_op jit(solution)/shard_map/reduce_scatter | solution.py:192
  440.9 1.9 fusion.40
  (97 shorter events, 11.8 us)
Async XLA Ops:
  7.2 390.7 %copy-start = (bf16[384,3072]{1,0:T(8,128)(2,1)S(1)}, bf16[384,3072]{1,0:T(8,128)(2,1)}, u32[]{:S(2)}) copy-start(bf16[384,3072]{1,0:T(8,128)(2,1)} %param.36) | copy-start | bytes 7077892
  7.2 35.5 %all-gather.10.cloned.1.call-start = ((), (), s32[]{:S(2)}) async-start(), calls=%async_computation.3 | async-start | bytes 1966080 | tf_op jit(solution)/shard_map/all_gather | solution.py:94
  7.9 189.7 %all-gather.12.cloned.1.call-start = ((), (), s32[]{:S(2)}) async-start(), calls=%async_computation.4 | async-start | bytes 12976128 | tf_op jit(solution)/shard_map/all_gather | solution.py:24
  42.7 3.9 copy-start.18
  46.6 2.4 copy-start.1
  46.6 2.4 copy-start.10
  46.6 2.4 copy-start.17
  46.6 8.1 %copy-start.5 = (bf16[3072,128]{1,0:T(8,128)(2,1)S(1)}, bf16[3072,128]{1,0:T(8,128)(2,1)}, u32[]{:S(2)}) copy-start(bf16[3072,128]{1,0:T(8,128)(2,1)} %param.28) | copy-start | bytes 2359300
  48.1 21.8 %copy-start.12 = (bf16[1,3,384]{2,1,0:T(4,128)(2,1)S(1)}, bf16[1,3,384]{2,1,0:T(4,128)(2,1)}, u32[]{:S(2)}) copy-start(bf16[1,3,384]{2,1,0:T(4,128)(2,1)} %param.39) | copy-start | bytes 6916
  48.1 23.2 %copy-start.11 = (bf16[1,3,512]{2,1,0:T(4,128)(2,1)S(1)}, bf16[1,3,512]{2,1,0:T(4,128)(2,1)}, u32[]{:S(2)}) copy-start(bf16[1,3,512]{2,1,0:T(4,128)(2,1)} %param.40) | copy-start | bytes 9220
  51.6 20.1 %copy-start.13 = (f32[3]{0:T(128)}, f32[3]{0:T(128)S(1)}, u32[]{:S(2)}) copy-start(f32[3]{0:T(128)S(1)} %get-tuple-element.66) | copy-start | bytes 40
  51.6 18.3 %collective-permute-start = (bf16[3,384]{1,0:T(4,128)(2,1)S(1)}, bf16[3,384]{1,0:T(4,128)(2,1)S(1)}, u32[]{:S(2)}, u32[]{:S(2)}) collective-permute-start(bf16[3,384]{1,0:T(4,128)(2,1)S(1)} %slice_bitcast_fusion.1), channel_id=1, source_target_pairs={{0,8},{8,16},{16,24},{24,32},{32,40},{40,48},{48,56},{56,64},{64,7... | collective-permute-start | bytes 6920 | tf_op jit(solution)/shard_map/ppermute | solution.py:19
  66.0 7.7 %copy-start.9 = (bf16[1,256,128]{2,1,0:T(8,128)(2,1)S(1)}, bf16[1,256,128]{2,1,0:T(8,128)(2,1)}, u32[]{:S(2)}) copy-start(bf16[1,256,128]{2,1,0:T(8,128)(2,1)} %param.37) | copy-start | bytes 196612
  66.1 5.2 %collective-permute-start.1 = (bf16[3,512]{1,0:T(4,128)(2,1)S(1)}, bf16[3,512]{1,0:T(4,128)(2,1)S(1)}, u32[]{:S(2)}, u32[]{:S(2)}) collective-permute-start(bf16[3,512]{1,0:T(4,128)(2,1)S(1)} %slice.136), channel_id=1, source_target_pairs={{0,8},{8,16},{16,24},{24,32},{32,40},{40,48},{48,56},{56,64},{64,7... | collective-permute-start | bytes 9224 | tf_op jit(solution)/shard_map/ppermute | solution.py:19
  71.3 24.4 %copy-start.4 = (f32[256,384]{0,1:T(8,128)}, f32[256,384]{0,1:T(8,128)S(1)}, u32[]{:S(2)}) copy-start(f32[256,384]{0,1:T(8,128)S(1)} %copy.58) | copy-start | bytes 1179652
  71.4 25.2 %copy-start.16 = (bf16[384]{0:T(512)(128)(2,1)S(1)}, bf16[384]{0:T(512)(128)(2,1)}, u32[]{:S(2)}) copy-start(bf16[384]{0:T(512)(128)(2,1)} %param.35) | copy-start | bytes 2308
  73.0 272.6 %all-gather.8.cloned.1.call-start = ((), (), s32[]{:S(2)}) async-start(), calls=%async_computation.1 | async-start | bytes 17301504 | tf_op jit(solution)/shard_map/all_gather | solution.py:163
  85.9 9.8 %copy-start.6 = (bf16[256,128]{0,1:T(8,128)(2,1)}, bf16[256,128]{0,1:T(8,128)(2,1)S(1)}, u32[]{:S(2)}) copy-start(bf16[256,128]{0,1:T(8,128)(2,1)S(1)} %fusion.63) | copy-start | bytes 196612
  96.5 344.3 %reduce-scatter.2.cloned.1.call-start = ((), (), s32[]{:S(2)}) async-start(), calls=%async_computation.2 | async-start | bytes 3932160 | tf_op jit(solution)/shard_map/reduce_scatter | solution.py:192
  98.6 20.3 %copy-start.15 = (f32[3]{0:T(128)S(1)}, f32[3]{0:T(128)}, u32[]{:S(2)}) copy-start(f32[3]{0:T(128)} %get-tuple-element.67) | copy-start | bytes 40
  199.2 146.5 %copy-start.7 = (bf16[256,2,64]{2,0,1:T(8,128)(2,1)S(1)}, bf16[256,2,64]{2,0,1:T(8,128)(2,1)}, u32[]{:S(2)}) copy-start(bf16[256,2,64]{2,0,1:T(8,128)(2,1)} %get-tuple-element.86) | copy-start | bytes 196612
  199.2 146.5 %copy-start.8 = (bf16[256,2,64]{2,0,1:T(8,128)(2,1)S(1)}, bf16[256,2,64]{2,0,1:T(8,128)(2,1)}, u32[]{:S(2)}) copy-start(bf16[256,2,64]{2,0,1:T(8,128)(2,1)} %get-tuple-element.87) | copy-start | bytes 196612
  397.9 2.7 copy-start.14
  397.9 4.4 copy-start.2
  400.6 40.2 %copy-start.3 = (bf16[1,256,768]{2,1,0:T(8,128)(2,1)S(1)}, bf16[1,256,768]{2,1,0:T(8,128)(2,1)}, u32[]{:S(2)}) copy-start(bf16[1,256,768]{2,1,0:T(8,128)(2,1)} %param.22) | copy-start | bytes 1179652
Sparse Core Ops, SparseCore 0:
  9.8 32.8 all-gather.9
  73.2 124.4 all-gather.11
  200.1 145.5 all-gather.7
  400.8 40.0 reduce-scatter.1
where the time goes:
time: 452 us; the launch traced here: 449 us
  waiting for transfers between devices  252 us (56%)
  blocking collectives  65.9 us (15%)
  matrix products  53.8 us (12%)
  other arithmetic  50.4 us (11%)
  between operations  14.9 us (3%)
  starting transfers between devices  6.45 us (1%)
  local copies, waits for them, and re-layouts  5.89 us (1%)
    all_gather x1, waiting for transfers between devices, shards(): piece = lax.all_gather(local_rows, 'seq', axis=0, tiled=True)  144 us
    all_gather x1, waiting for transfers between devices, prefix(): gathered = jax.tree.map(lambda a: lax.all_gather(a, axis), part)  39.1 us
    all_gather x1, blocking collectives, prefix(): gathered = jax.tree.map(lambda a: lax.all_gather(a, axis), part)  37.4 us
    reduce_scatter x1, waiting for transfers between devices, shards(): summed = lax.psum_scatter(term, 'mp', scatter_dimension=1, tiled=True)  36.7 us
    all_gather x1, waiting for transfers between devices, shards(): whole = lax.all_gather(own_rows, 'mp', axis=1, tiled=True)  31.7 us
    dot_general x1, matrix products, shards(): jnp.einsum('qhd,kd->hqk', query, piece[:, :HD], preferred_element_type=jn...  17.5 us
    dot_general x1, matrix products, shards(): jnp.einsum('hqk,kd->hqd', weights.astype(jnp.bfloat16), piece[:, HD:2 * H...  17.1 us
    reduce_sum x1, other arithmetic, shards(): total = jnp.sum(weights, axis=-1)  15.6 us
  transfers between devices with their start and end apart: 6, of which 4 were waited for; matrix products, arithmetic and copies ran while one was open for 10% of the time, Pallas kernels for 0%

commit v1 on v0

--- a/solution.py
+++ b/solution.py
@@ -1,3 +1,4 @@
+import functools
 import jax
 import jax.numpy as jnp
 from jax import lax
@@ -11,6 +12,37 @@
 epsilon = 1e-05
 rope_base = 100000000000.0
 negative = -1e30
+
+
+def list_the_table(vals, on_dim):
+    vals = jnp.moveaxis(vals, 0, on_dim)
+    extra = vals.shape
+    return vals.reshape(*extra[:on_dim], extra[on_dim] * extra[on_dim + 1], *extra[on_dim + 2 :])
+
+
+def list_the_lanes(u, ax_name, d_out):
+    total_devices = jax.lax.axis_size(ax_name)
+    a_next = range(total_devices)
+    opened = map(lambda h: (h, (h + 1) % total_devices), a_next)
+    chunks = list(opened)
+    trail = [(ix, dev_i) for dev_i, ix in chunks]
+    part_now, last = ([], [])
+    for nth in [*range(total_devices - 1)]:
+        if nth % 2 == 0:
+            w_next = jax.lax.ppermute(part_now[-1] if part_now else u, ax_name, chunks)
+            part_now.append(w_next)
+        else:
+            outer = jax.lax.ppermute(last[-1] if last else u, ax_name, trail)
+            last.append(outer)
+    o_now = jnp.stack([*part_now[::-1], u, *last])
+    z_new = jax.lax.axis_index(ax_name)
+    aux = len(part_now)
+    all_values = z_new - aux
+    o_now = o_now[(jnp.arange(total_devices) - all_values) % total_devices]
+    return list_the_table(o_now, d_out)
+
+
+perform_packet_by_axis = functools.partial(list_the_lanes, ax_name="mp", d_out=1)
 
 
 def shifted(block, axis, distance):
@@ -110,7 +142,7 @@
     kv_all, bc_all, cache_all = (
         lax.all_gather(kv_block, "mp", axis=1, tiled=True),
         lax.all_gather(bc_block, "mp", axis=1, tiled=True),
-        lax.all_gather(cache[0], "mp", axis=1, tiled=True),
+        perform_packet_by_axis(cache[0]),
     )
     inner = jnp.einsum("td,dkc->tkc", normed, w_inner, preferred_element_type=jnp.float32).astype(
         jnp.bfloat16

time: 452 us -> 452 us (level)
  blocking collectives: 65.9 us -> 57.2 us
    all_gather x1 -> x0, blocking collectives: 9.37 us -> none  [shards(): lax.all_gather(cache[0], 'mp', axis=1, tiled=True)]
    ppermute x0 -> x3, waiting for transfers between devices: none -> 5.01 us  [the longest x2 5 us: list_the_lanes(): w_next = jax.lax.ppermute(part_now[-1] if part_now else u, ax_name, chunks)]
    all_gather x1, waiting for transfers between devices: 39.1 us -> 34.6 us  [prefix(): gathered = jax.tree.map(lambda a: lax.all_gather(a, axis), part)]
  transfers between devices with their start and end apart: 6 -> 9, of which waited for: 4 -> 6; matrix products, arithmetic and copies ran while one was open for 10% -> 11% of each run, Pallas kernels for 0% -> 0%
where the time goes in v1:
time: 452 us; the launch traced here: 449 us
  waiting for transfers between devices  252 us (56%)
  blocking collectives  57.2 us (13%)
  other arithmetic  54 us (12%)
  matrix products  53.6 us (12%)
  between operations  14.9 us (3%)
  starting transfers between devices  9.26 us (2%)
  local copies, waits for them, and re-layouts  7.74 us (2%)
    all_gather x1, waiting for transfers between devices, shards(): piece = lax.all_gather(local_rows, 'seq', axis=0, tiled=True)  143 us
    all_gather x1, blocking collectives, prefix(): gathered = jax.tree.map(lambda a: lax.all_gather(a, axis), part)  38.1 us
    reduce_scatter x1, waiting for transfers between devices, shards(): summed = lax.psum_scatter(term, 'mp', scatter_dimension=1, tiled=True)  36.7 us
    all_gather x1, waiting for transfers between devices, prefix(): gathered = jax.tree.map(lambda a: lax.all_gather(a, axis), part)  34.6 us
    all_gather x1, waiting for transfers between devices, shards(): whole = lax.all_gather(own_rows, 'mp', axis=1, tiled=True)  31.7 us
    dot_general x1, matrix products, shards(): jnp.einsum('qhd,kd->hqk', query, piece[:, :HD], preferred_element_type=jn...  17.3 us
    dot_general x1, matrix products, shards(): jnp.einsum('hqk,kd->hqd', weights.astype(jnp.bfloat16), piece[:, HD:2 * H...  17.1 us
    reduce_sum x1, other arithmetic, shards(): total = jnp.sum(weights, axis=-1)  15.6 us
  transfers between devices with their start and end apart: 9, of which 6 were waited for; matrix products, arithmetic and copies ran while one was open for 11% of the time, Pallas kernels for 0%

profile of v1, /device:TPU:1, one launch (start us, length us, event | category | flops | bytes accessed | tf_op | source)
XLA Modules:
  0.0 449.0 jit_solution(14697746274241853691)
XLA Ops:
  11.0 31.7 %all-gather.9.cloned.1.call-done = bf16[1,256,3072]{2,1,0:T(8,128)(2,1)} async-done(((bf16[1,256,768]{2,1,0:T(8,128)(2,1)}), bf16[1,256,3072]{2,1,0:T(8,128)(2,1)}) %all-gather.9.cloned.1.call-update) | async-done | bytes 1572880 | tf_op jit(solution)/shard_map/all_gather | solution.py:126
  42.7 1.9 fusion.9
  44.7 1.9 fusion.11
  46.6 1.4 fusion.13
  51.5 3.1 collective-permute-start.3
  54.7 2.0 convolution_convert_fusion
  56.6 9.4 %all_gather.25 = bf16[256,512]{1,0:T(8,128)(2,1)S(1)} all-gather(bf16[256,128]{1,0:T(8,128)(2,1)S(1)} %convolution_convert_fusion), channel_id=1, replica_groups=mesh['seq'=32,'mp'=4,'req'=2] {'mp'}, dimensions={1}, use_global_device_ids=true | all-gather | bytes 327680 | tf_op jit(solution)/shard_map/all_gather | solution.py:144
  66.0 3.2 collective-permute-start.4
  71.7 1.3 fusion.46
  73.5 2.4 collective-permute-start.2
  78.1 4.1 collective-permute-done.1
  83.1 1.3 gather_fusion
  85.5 2.3 fusion.102
  89.4 9.8 %all_gather.23 = bf16[256,512]{0,1:T(8,128)(2,1)S(1)} all-gather(bf16[256,128]{0,1:T(8,128)(2,1)S(1)} %fusion.63), channel_id=1, replica_groups=mesh['seq'=32,'mp'=4,'req'=2] {'mp'}, dimensions={1}, use_global_device_ids=true | all-gather | bytes 327680 | tf_op jit(solution)/shard_map/all_gather | solution.py:143
  101.5 1.9 multiply_cosine_fusion
  103.5 15.5 %and_or_fusion = pred[256,16384]{0,1:T(8,128)(4,1)} fusion(s32[256]{0:T(256)S(1)} %iota_add_fusion, s32[16384]{0:T(1024)S(1)} %fusion.82, pred[16384]{0:T(1024)(128)(4,1)S(1)} %get-tuple-element.110, pred[16384]{0:T(1024)(128)(4,1)S(1)} %get-tuple-element.109), kind=kLoop, calls=%fused_computation.10 | loop fusion | flops 12582912 | bytes 4293632 | tf_op jit(solution)/shard_map/or | solution.py:205
  119.9 2.6 fusion.103
  122.8 38.1 %all-gather.2 = f32[32,1,3]{2,1,0:T(1,128)} all-gather(f32[1,1,3]{2,1,0:T(1,128)S(1)} %bitcast.194), channel_id=1, replica_groups=mesh['seq'=32,'mp'=4,'req'=2] {'seq'}, dimensions={0}, use_global_device_ids=true | all-gather | bytes 396 | tf_op jit(solution)/shard_map/all_gather | solution.py:56
  160.9 1.8 subtract_convert_fusion
  163.1 34.6 %all-gather.11.cloned.1.call-done = f32[96,128,256]{2,1,0:T(8,128)} async-done(((f32[3,128,256]{2,1,0:T(8,128)}), f32[96,128,256]{2,1,0:T(8,128)}) %all-gather.11.cloned.1.call-update) | async-done | bytes 12582928 | tf_op jit(solution)/shard_map/all_gather | solution.py:56
  197.9 1.5 convolution_multiply_fusion
  199.5 2.5 multiply_reduce_fusion
  202.2 143.2 %all-gather.7.cloned.1.call-done = bf16[16384,512]{0,1:T(8,128)(2,1)} async-done(((bf16[512,512]{0,1:T(8,128)(2,1)}), bf16[16384,512]{0,1:T(8,128)(2,1)}) %all-gather.7.cloned.1.call-update) | async-done | bytes 16777232 | tf_op jit(solution)/shard_map/all_gather | solution.py:195
  345.4 17.3 %fusion = (f32[2,256]{1,0:T(2,128)S(1)}, f32[16384,256,2]{1,0,2:T(8,128)}) fusion(pred[256,16384]{0,1:T(8,128)(4,1)} %and_or_fusion, bf16[256,2,64]{2,0,1:T(8,128)(2,1)S(1)} %copy-done.9, bf16[256,2,64]{2,0,1:T(8,128)(2,1)S(1)} %copy-done.8, bf16[16384,512]{0,1:T(8,128)(2,1)} %all-gather.7.cloned.1.call-done, s32[]{:T(128)S(6)} %select_n.132), kind=kOutput, calls=%fused_computation.5 | convolution fusion | flops 2172911104 | bytes 42076164 | tf_op jit(solution)/shard_map/qhd,kd->hqk/dot_general | solution.py:207
  362.7 15.6 %fusion.1 = f32[2,256]{1,0:T(2,128)S(1)} fusion(f32[16384,256,2]{1,0,2:T(8,128)} %get-tuple-element.104, f32[2,256]{1,0:T(2,128)S(1)} %broadcast_maximum_fusion, pred[256,16384]{0,1:T(8,128)(4,1)} %and_or_fusion), kind=kLoop, calls=%fused_computation.6 | loop fusion | flops 41942528 | bytes 37752832 | tf_op jit(solution)/shard_map/reduce_sum | solution.py:212
  378.3 17.1 %fusion.27 = bf16[256,2,128]{0,2,1:T(8,128)(2,1)S(1)} fusion(f32[16384,256,2]{1,0,2:T(8,128)} %get-tuple-element.104, f32[2,256]{1,0:T(2,128)S(1)} %broadcast_maximum_fusion, pred[256,16384]{0,1:T(8,128)(4,1)} %and_or_fusion, bf16[16384,512]{0,1:T(8,128)(2,1)} %all-gather.7.cloned.1.call-done, s32[]{:T(128)S(6)} %add.255, f32[256,2]{0,1:T(2,128)S(1)} %bitcast.193), kind=kOutput, calls=%fused_computation.33 | convolution fusion | flops 2189557760 | bytes 42078212 | tf_op jit(solution)/shard_map/hqk,kd->hqd/dot_general | solution.py:213
  395.4 2.0 fusion.104
  397.5 2.7 convolution_add_fusion
  400.2 1.6 copy.64
  401.9 1.9 add_bitcast_fusion
  403.7 36.7 %reduce-scatter.2.cloned.1.call-done = f32[256,768]{1,0:T(8,128)} async-done(((f32[256,3072]{1,0:T(8,128)}), f32[256,768]{1,0:T(8,128)}) %reduce-scatter.2.cloned.1.call-update) | async-done | bytes 786448 | tf_op jit(solution)/shard_map/reduce_scatter | solution.py:224
  440.5 1.9 fusion.40
  (114 shorter events, 19.7 us)
Async XLA Ops:
  7.2 390.3 %copy-start = (bf16[384,3072]{1,0:T(8,128)(2,1)S(1)}, bf16[384,3072]{1,0:T(8,128)(2,1)}, u32[]{:S(2)}) copy-start(bf16[384,3072]{1,0:T(8,128)(2,1)} %param.36) | copy-start | bytes 7077892
  7.2 35.5 %all-gather.9.cloned.1.call-start = ((), (), s32[]{:S(2)}) async-start(), calls=%async_computation.3 | async-start | bytes 1966080 | tf_op jit(solution)/shard_map/all_gather | solution.py:126
  7.9 189.8 %all-gather.11.cloned.1.call-start = ((), (), s32[]{:S(2)}) async-start(), calls=%async_computation.4 | async-start | bytes 12976128 | tf_op jit(solution)/shard_map/all_gather | solution.py:56
  42.7 3.9 copy-start.22
  46.6 2.4 copy-start.1
  46.6 2.4 copy-start.13
  46.6 2.4 copy-start.21
  46.6 8.0 %copy-start.6 = (bf16[3072,128]{1,0:T(8,128)(2,1)S(1)}, bf16[3072,128]{1,0:T(8,128)(2,1)}, u32[]{:S(2)}) copy-start(bf16[3072,128]{1,0:T(8,128)(2,1)} %param.28) | copy-start | bytes 2359300
  48.1 21.8 %copy-start.16 = (bf16[1,3,384]{2,1,0:T(4,128)(2,1)S(1)}, bf16[1,3,384]{2,1,0:T(4,128)(2,1)}, u32[]{:S(2)}) copy-start(bf16[1,3,384]{2,1,0:T(4,128)(2,1)} %param.39) | copy-start | bytes 6916
  48.1 23.2 %copy-start.15 = (bf16[1,3,512]{2,1,0:T(4,128)(2,1)S(1)}, bf16[1,3,512]{2,1,0:T(4,128)(2,1)}, u32[]{:S(2)}) copy-start(bf16[1,3,512]{2,1,0:T(4,128)(2,1)} %param.40) | copy-start | bytes 9220
  51.5 20.2 %copy-start.18 = (f32[3]{0:T(128)}, f32[3]{0:T(128)S(1)}, u32[]{:S(2)}) copy-start(f32[3]{0:T(128)S(1)} %get-tuple-element.66) | copy-start | bytes 40
  51.5 18.3 %collective-permute-start.3 = (bf16[3,384]{1,0:T(4,128)(2,1)S(1)}, bf16[3,384]{1,0:T(4,128)(2,1)S(1)}, u32[]{:S(2)}, u32[]{:S(2)}) collective-permute-start(bf16[3,384]{1,0:T(4,128)(2,1)S(1)} %slice_bitcast_fusion.1), channel_id=1, source_target_pairs={{0,8},{8,16},{16,24},{24,32},{32,40},{40,48},{48,56},{56,64},{64,7... | collective-permute-start | bytes 6920 | tf_op jit(solution)/shard_map/ppermute | solution.py:51
  66.0 7.1 %copy-start.10 = (bf16[1,256,128]{2,1,0:T(8,128)(2,1)S(1)}, bf16[1,256,128]{2,1,0:T(8,128)(2,1)}, u32[]{:S(2)}) copy-start(bf16[1,256,128]{2,1,0:T(8,128)(2,1)} %param.37) | copy-start | bytes 196612
  66.0 5.3 %collective-permute-start.4 = (bf16[3,512]{1,0:T(4,128)(2,1)S(1)}, bf16[3,512]{1,0:T(4,128)(2,1)S(1)}, u32[]{:S(2)}, u32[]{:S(2)}) collective-permute-start(bf16[3,512]{1,0:T(4,128)(2,1)S(1)} %slice.138), channel_id=1, source_target_pairs={{0,8},{8,16},{16,24},{24,32},{32,40},{40,48},{48,56},{56,64},{64,7... | collective-permute-start | bytes 9224 | tf_op jit(solution)/shard_map/ppermute | solution.py:51
  71.3 16.5 %copy-start.4 = (f32[256,384]{0,1:T(8,128)}, f32[256,384]{0,1:T(8,128)S(1)}, u32[]{:S(2)}) copy-start(f32[256,384]{0,1:T(8,128)S(1)} %copy.58) | copy-start | bytes 1179652
  73.0 272.4 %all-gather.7.cloned.1.call-start = ((), (), s32[]{:S(2)}) async-start(), calls=%async_computation.1 | async-start | bytes 17301504 | tf_op jit(solution)/shard_map/all_gather | solution.py:195
  73.1 4.4 collective-permute-start
  73.5 4.6 %collective-permute-start.2 = (bf16[256,128]{1,0:T(8,128)(2,1)S(1)}, bf16[256,128]{1,0:T(8,128)(2,1)S(1)}, u32[]{:S(2)}, u32[]{:S(2)}) collective-permute-start(bf16[256,128]{1,0:T(8,128)(2,1)S(1)} %bitcast.181), channel_id=1, source_target_pairs={{2,0},{4,2},{6,4},{0,6},{3,1},{5,3},{7,5},{1,7},{10,8},{12,10},{14... | collective-permute-start | bytes 196616 | tf_op jit(solution)/shard_map/ppermute | solution.py:35
  76.5 23.6 %copy-start.14 = (f32[256]{0:T(256)}, f32[256]{0:T(256)S(1)}, u32[]{:S(2)}) copy-start(f32[256]{0:T(256)S(1)} %add_convert_fusion.1) | copy-start | bytes 3076
  77.5 4.6 %copy-start.11 = (bf16[256,128]{1,0:T(8,128)(2,1)}, bf16[256,128]{1,0:T(8,128)(2,1)S(1)}, u32[]{:S(2)}) copy-start(bf16[256,128]{1,0:T(8,128)(2,1)S(1)} %collective-permute-done) | copy-start | bytes 196612
  77.5 4.6 %collective-permute-start.1 = (bf16[256,128]{1,0:T(8,128)(2,1)S(1)}, bf16[256,128]{1,0:T(8,128)(2,1)S(1)}, u32[]{:S(2)}, u32[]{:S(2)}) collective-permute-start(bf16[256,128]{1,0:T(8,128)(2,1)S(1)} %collective-permute-done), channel_id=1, source_target_pairs={{0,2},{2,4},{4,6},{6,0},{1,3},{3,5},{5,7},{7,1},{8,10},{10,12},{12... | collective-permute-start | bytes 196616 | tf_op jit(solution)/shard_map/ppermute | solution.py:32
  78.1 4.1 copy-start.12
  84.4 17.2 %copy-start.17 = (f32[64]{0:T(128)S(1)}, f32[64]{0:T(128)}, u32[]{:S(2)}) copy-start(f32[64]{0:T(128)} %multiply_power_fusion) | copy-start | bytes 772
  87.8 31.2 %copy-start.5 = (f32[256,1,384]{2,0,1:T(8,128)S(1)}, f32[256,1,384]{2,0,1:T(8,128)}, u32[]{:S(2)}) copy-start(f32[256,1,384]{2,0,1:T(8,128)} %get-tuple-element.88) | copy-start | bytes 1179652
  88.8 0.6 copy-start.7
  100.1 340.4 %reduce-scatter.2.cloned.1.call-start = ((), (), s32[]{:S(2)}) async-start(), calls=%async_computation.2 | async-start | bytes 3932160 | tf_op jit(solution)/shard_map/reduce_scatter | solution.py:224
  103.5 19.3 %copy-start.20 = (f32[3]{0:T(128)S(1)}, f32[3]{0:T(128)}, u32[]{:S(2)}) copy-start(f32[3]{0:T(128)} %get-tuple-element.67) | copy-start | bytes 40
  199.5 146.0 %copy-start.8 = (bf16[256,2,64]{2,0,1:T(8,128)(2,1)S(1)}, bf16[256,2,64]{2,0,1:T(8,128)(2,1)}, u32[]{:S(2)}) copy-start(bf16[256,2,64]{2,0,1:T(8,128)(2,1)} %get-tuple-element.86) | copy-start | bytes 196612
  199.5 146.0 %copy-start.9 = (bf16[256,2,64]{2,0,1:T(8,128)(2,1)S(1)}, bf16[256,2,64]{2,0,1:T(8,128)(2,1)}, u32[]{:S(2)}) copy-start(bf16[256,2,64]{2,0,1:T(8,128)(2,1)} %get-tuple-element.87) | copy-start | bytes 196612
  397.5 2.8 copy-start.19
  397.5 4.4 copy-start.2
  400.2 40.3 %copy-start.3 = (bf16[1,256,768]{2,1,0:T(8,128)(2,1)S(1)}, bf16[1,256,768]{2,1,0:T(8,128)(2,1)}, u32[]{:S(2)}) copy-start(bf16[1,256,768]{2,1,0:T(8,128)(2,1)} %param.22) | copy-start | bytes 1179652
Sparse Core Ops, SparseCore 0:
  9.8 32.8 all-gather.8
  73.1 124.4 all-gather.10
  200.2 145.2 all-gather.6
  400.3 40.0 reduce-scatter.1
